TPU v7x, 32 devices: a whole 2x2x4 slice. The times are simulated.
32 devices in a mesh: dp: 32 (over z, y, x, core).
Axes of the slice: x: 2, y: 2, z: 4, core: 2. Of those that a mesh axis runs over, the one named last changes fastest.
Arguments:
- tokens: bfloat16 [4096, 1024], P('dp'), may hold values from -6 to 6
- lengths: int32 [32, 2], P('dp'), may hold values from 1 to 64, as said below
- cotangent: bfloat16 [4096, 1024], P('dp'), may hold values from -6 to 6
- norm1_gain: bfloat16 [1024], P('dp'), may hold values from 0.5 to 1.5
- norm1_shift: bfloat16 [1024], P('dp'), may hold values from -3 to 3
- joint_weight: bfloat16 [1024, 3072], P('dp'), may hold values from -0.1875 to 0.1875
- query_bias: bfloat16 [1024], P('dp'), may hold values from -3 to 3
- value_bias: bfloat16 [1024], P('dp'), may hold values from -3 to 3
- output_weight: bfloat16 [1024, 1024], P('dp'), may hold values from -0.5 to 0.5
- output_bias: bfloat16 [1024], P('dp'), may hold values from -3 to 3
- norm2_gain: bfloat16 [1024], P('dp'), may hold values from 0.5 to 1.5
- norm2_shift: bfloat16 [1024], P('dp'), may hold values from -3 to 3
- expand_weight: bfloat16 [1024, 4096], P('dp'), may hold values from -0.1875 to 0.1875
- expand_bias: bfloat16 [4096], P('dp'), may hold values from -3 to 3
- reduce_weight: bfloat16 [4096, 1024], P('dp'), may hold values from -0.09375 to 0.09375
- reduce_bias: bfloat16 [1024], P('dp'), may hold values from -3 to 3
Outputs:
- layer_output: bfloat16 [4096, 1024], P('dp')
- grad_tokens: float32 [4096, 1024], P('dp')
- grad_norm1_gain: float32 [1024], P('dp')
- grad_norm1_shift: float32 [1024], P('dp')
- grad_joint_weight: float32 [1024, 3072], P('dp')
- grad_query_bias: float32 [1024], P('dp')
- grad_value_bias: float32 [1024], P('dp')
- grad_output_weight: float32 [1024, 1024], P('dp')
- grad_output_bias: float32 [1024], P('dp')
- grad_norm2_gain: float32 [1024], P('dp')
- grad_norm2_shift: float32 [1024], P('dp')
- grad_expand_weight: float32 [1024, 4096], P('dp')
- grad_expand_bias: float32 [4096], P('dp')
- grad_reduce_weight: float32 [4096, 1024], P('dp')
- grad_reduce_bias: float32 [1024], P('dp')
Inputs may be any that keep to these rules, and one draw needn't show every extreme that they name: On every device one sequence has the largest length 64, and on one device all sequences have it; the lengths of a device sum to at most 128.
All inputs are finite; a program needn't handle non-finite values.
Results may differ from a plain program's by a relative error of at most 0.011.
Values may be sent and summed in bfloat16 or wider, within the bound.
A program may use at most 192 MiB of HBM per device.

v0:
```python
import jax
import jax.numpy as jnp
from jax import lax
from jax.sharding import PartitionSpec as P

HEADS = 16


EPSILON = 1e-05
TANH_SCALE = 0.7978845608028654
CUBIC_TERM = 0.044715


def layer_norm(row_data, gain_vector, shift_vector):
    average = jnp.mean(row_data, axis=-1, keepdims=True)
    centred = row_data - average
    spread = jnp.mean(centred * centred, axis=-1, keepdims=True)
    return centred * lax.rsqrt(spread + EPSILON) * gain_vector + shift_vector


def activation(values_in):
    return (
        0.5
        * values_in
        * (
            1.0
            + jnp.tanh(TANH_SCALE * (values_in + CUBIC_TERM * values_in * values_in * values_in))
        )
    )


def contract(pattern, first_op, second_op):
    return jnp.einsum(pattern, first_op, second_op, preferred_element_type=jnp.float32)


def transposed_left(first_op, second_op):
    return lax.dot_general(
        first_op, second_op, (((0,), (0,)), ((), ())), preferred_element_type=jnp.float32
    )


def transposed_right(first_op, second_op):
    return lax.dot_general(
        first_op, second_op, (((1,), (1,)), ((), ())), preferred_element_type=jnp.float32
    )


def flatten_lanes(matrix):
    return matrix.reshape(-1, 128)


def slot_mask(lengths_row, row_count):
    seq_ends = jnp.cumsum(lengths_row)
    position = jnp.arange(row_count, dtype=jnp.int32)
    segment = jnp.sum((position[:, None] >= seq_ends[None, :]).astype(jnp.int32), axis=1)
    live_rows = position < seq_ends[-1]
    segment = jnp.where(live_rows, segment, row_count + position)
    allowed = (segment[:, None] == segment[None, :]) & (position[:, None] >= position[None, :])
    return (allowed, live_rows.astype(jnp.float32))


def masked_scores(query_heads, key_heads, allowed):
    score_scale = query_heads.shape[2] ** (-0.5)
    scores = contract("qhd,khd->hqk", query_heads, key_heads) * score_scale
    return jnp.where(allowed[None, :, :], scores, -1e30)


def forward(tokens, lengths_row, attn_params, ffn_params):
    gain_first, shift_first, joint_weight, query_bias, value_bias, output_weight, output_bias = (
        attn_params
    )
    gain_second, shift_second, expand_weight, expand_bias, reduce_weight, reduce_bias = ffn_params
    row_count, model_width = tokens.shape
    head_size = model_width // HEADS
    allowed, live_rows = slot_mask(lengths_row, row_count)
    residual = tokens.astype(jnp.float32)
    first_normed = layer_norm(
        residual, gain_first.astype(jnp.float32), shift_first.astype(jnp.float32)
    ).astype(jnp.bfloat16)
    packed = jnp.dot(first_normed, joint_weight, preferred_element_type=jnp.float32)
    query_heads = (
        (packed[:, :model_width] + query_bias.astype(jnp.float32))
        .astype(jnp.bfloat16)
        .reshape(row_count, HEADS, head_size)
    )
    key_heads = (
        packed[:, model_width : 2 * model_width]
        .astype(jnp.bfloat16)
        .reshape(row_count, HEADS, head_size)
    )
    value_heads = (
        (packed[:, 2 * model_width :] + value_bias.astype(jnp.float32))
        .astype(jnp.bfloat16)
        .reshape(row_count, HEADS, head_size)
    )
    scores = masked_scores(query_heads, key_heads, allowed)
    row_top = jnp.max(scores, axis=-1, keepdims=True)
    logsum = row_top + jnp.log(jnp.sum(jnp.exp(scores - row_top), axis=-1, keepdims=True))
    weights = jnp.exp(scores - logsum).astype(jnp.bfloat16)
    context = (
        contract("hqk,khd->qhd", weights, value_heads)
        .astype(jnp.bfloat16)
        .reshape(row_count, model_width)
    )
    middle = (
        residual
        + jnp.dot(context, output_weight, preferred_element_type=jnp.float32)
        + output_bias.astype(jnp.float32)
    )
    second_normed = layer_norm(
        middle, gain_second.astype(jnp.float32), shift_second.astype(jnp.float32)
    ).astype(jnp.bfloat16)
    before = jnp.dot(
        second_normed, expand_weight, preferred_element_type=jnp.float32
    ) + expand_bias.astype(jnp.float32)
    active = activation(before).astype(jnp.bfloat16)
    block_final = (
        middle
        + jnp.dot(active, reduce_weight, preferred_element_type=jnp.float32)
        + reduce_bias.astype(jnp.float32)
    )
    stored_state = (
        residual,
        first_normed,
        query_heads,
        key_heads,
        value_heads,
        allowed,
        live_rows,
        logsum,
        context,
        middle,
        second_normed,
        before,
        active,
    )
    return (block_final.astype(jnp.bfloat16), stored_state)


def backward(stored_state, cotangent, attn_params, ffn_params):
    (
        residual,
        first_normed,
        query_heads,
        key_heads,
        value_heads,
        allowed,
        live_rows,
        logsum,
        context,
        middle,
        second_normed,
        before,
        active,
    ) = stored_state
    gain_first, shift_first, joint_weight, query_bias, value_bias, output_weight, output_bias = (
        attn_params
    )
    gain_second, shift_second, expand_weight, expand_bias, reduce_weight, reduce_bias = ffn_params
    row_count, model_width = residual.shape
    head_size = model_width // HEADS
    score_scale = head_size ** (-0.5)
    grad_final = cotangent.astype(jnp.float32) * live_rows[:, None]
    grad_final_low = grad_final.astype(jnp.bfloat16)
    grad_reduce_bias = jnp.sum(grad_final, axis=0)
    grad_active = transposed_right(grad_final_low, reduce_weight)
    unused_value, curve_back = jax.vjp(activation, before)
    grad_before = curve_back(grad_active)[0]
    grad_expand_bias = jnp.sum(grad_before, axis=0)
    grad_before_low = grad_before.astype(jnp.bfloat16)
    grad_second_normed = transposed_right(grad_before_low, expand_weight)
    unused_norm, second_back = jax.vjp(
        layer_norm, middle, gain_second.astype(jnp.float32), shift_second.astype(jnp.float32)
    )
    grad_middle_norm, grad_gain_second, grad_shift_second = second_back(grad_second_normed)
    grad_middle = grad_final + grad_middle_norm
    grad_middle_low = grad_middle.astype(jnp.bfloat16)
    grad_output_bias = jnp.sum(grad_middle, axis=0)
    grad_context = (
        transposed_right(grad_middle_low, output_weight)
        .astype(jnp.bfloat16)
        .reshape(row_count, HEADS, head_size)
    )
    scores = masked_scores(query_heads, key_heads, allowed)
    probs = jnp.exp(scores - logsum)
    weights = probs.astype(jnp.bfloat16)
    grad_probs = contract("qhd,khd->hqk", grad_context, value_heads)
    grad_values = contract("hqk,qhd->khd", weights, grad_context)
    centre = jnp.sum(probs * grad_probs, axis=-1, keepdims=True)
    grad_scores = (probs * (grad_probs - centre) * score_scale).astype(jnp.bfloat16)
    grad_query = contract("hqk,khd->qhd", grad_scores, key_heads).reshape(row_count, model_width)
    grad_keys = contract("hqk,qhd->khd", grad_scores, query_heads).reshape(row_count, model_width)
    grad_values = grad_values.reshape(row_count, model_width)
    grad_query_bias = jnp.sum(grad_query, axis=0)
    grad_value_bias = jnp.sum(grad_values, axis=0)
    grad_packed = jnp.concatenate([grad_query, grad_keys, grad_values], axis=1).astype(jnp.bfloat16)
    grad_first_normed = transposed_right(grad_packed, joint_weight)
    unused_first, first_back = jax.vjp(
        layer_norm, residual, gain_first.astype(jnp.float32), shift_first.astype(jnp.float32)
    )
    grad_tokens_norm, grad_gain_first, grad_shift_first = first_back(grad_first_normed)
    grad_tokens = grad_middle + grad_tokens_norm
    ffn_factors = (second_normed, grad_before_low, active, grad_final_low)
    ffn_small = (grad_gain_second, grad_shift_second, grad_expand_bias, grad_reduce_bias)
    attn_factors = (first_normed, grad_packed, context, grad_middle_low)
    attn_small = (
        grad_gain_first,
        grad_shift_first,
        grad_query_bias,
        grad_value_bias,
        grad_output_bias,
    )
    return (grad_tokens, ffn_factors, ffn_small, attn_factors, attn_small)


def gather_attention(
    norm1_gain,
    norm1_shift,
    joint_weight,
    query_bias,
    value_bias,
    output_weight,
    output_bias,
    model_width,
):
    pieces = (
        lax.all_gather(norm1_gain, "dp", axis=0, tiled=True),
        lax.all_gather(norm1_shift, "dp", axis=0, tiled=True),
        lax.all_gather(flatten_lanes(joint_weight), "dp", axis=0, tiled=True),
        lax.all_gather(query_bias, "dp", axis=0, tiled=True),
        lax.all_gather(value_bias, "dp", axis=0, tiled=True),
        lax.all_gather(flatten_lanes(output_weight), "dp", axis=0, tiled=True),
        lax.all_gather(output_bias, "dp", axis=0, tiled=True),
    )
    return (
        pieces[0],
        pieces[1],
        pieces[2].reshape(model_width, 3 * model_width),
        pieces[3],
        pieces[4],
        pieces[5].reshape(model_width, model_width),
        pieces[6],
    )


def gather_feedforward(
    norm2_gain,
    norm2_shift,
    expand_weight,
    expand_bias,
    reduce_weight,
    reduce_bias,
    model_width,
    hidden_width,
):
    pieces = (
        lax.all_gather(norm2_gain, "dp", axis=0, tiled=True),
        lax.all_gather(norm2_shift, "dp", axis=0, tiled=True),
        lax.all_gather(flatten_lanes(expand_weight), "dp", axis=0, tiled=True),
        lax.all_gather(expand_bias, "dp", axis=0, tiled=True),
        lax.all_gather(flatten_lanes(reduce_weight), "dp", axis=0, tiled=True),
        lax.all_gather(reduce_bias, "dp", axis=0, tiled=True),
    )
    return (
        pieces[0],
        pieces[1],
        pieces[2].reshape(model_width, hidden_width),
        pieces[3],
        pieces[4].reshape(hidden_width, model_width),
        pieces[5],
    )


def on_device(
    tokens,
    lengths,
    cotangent,
    norm1_gain,
    norm1_shift,
    joint_weight,
    query_bias,
    value_bias,
    output_weight,
    output_bias,
    norm2_gain,
    norm2_shift,
    expand_weight,
    expand_bias,
    reduce_weight,
    reduce_bias,
):
    model_width = tokens.shape[1]
    hidden_width = expand_weight.shape[1]
    attn_params = gather_attention(
        norm1_gain,
        norm1_shift,
        joint_weight,
        query_bias,
        value_bias,
        output_weight,
        output_bias,
        model_width,
    )
    ffn_params = gather_feedforward(
        norm2_gain,
        norm2_shift,
        expand_weight,
        expand_bias,
        reduce_weight,
        reduce_bias,
        model_width,
        hidden_width,
    )
    layer_output, stored_state = forward(tokens, lengths[0], attn_params, ffn_params)
    attn_pieces = (
        lax.all_gather(norm1_gain, "dp", axis=0, tiled=True),
        lax.all_gather(norm1_shift, "dp", axis=0, tiled=True),
        lax.all_gather(flatten_lanes(joint_weight), "dp", axis=0, tiled=True),
        lax.all_gather(query_bias, "dp", axis=0, tiled=True),
        lax.all_gather(value_bias, "dp", axis=0, tiled=True),
        lax.all_gather(flatten_lanes(output_weight), "dp", axis=0, tiled=True),
        lax.all_gather(output_bias, "dp", axis=0, tiled=True),
    )
    attn_again = (
        attn_pieces[0],
        attn_pieces[1],
        attn_pieces[2].reshape(model_width, 3 * model_width),
        attn_pieces[3],
        attn_pieces[4],
        attn_pieces[5].reshape(model_width, model_width),
        attn_pieces[6],
    )
    ffn_pieces = (
        lax.all_gather(norm2_gain, "dp", axis=0, tiled=True),
        lax.all_gather(norm2_shift, "dp", axis=0, tiled=True),
        lax.all_gather(flatten_lanes(expand_weight), "dp", axis=0, tiled=True),
        lax.all_gather(expand_bias, "dp", axis=0, tiled=True),
        lax.all_gather(flatten_lanes(reduce_weight), "dp", axis=0, tiled=True),
        lax.all_gather(reduce_bias, "dp", axis=0, tiled=True),
    )
    ffn_again = (
        ffn_pieces[0],
        ffn_pieces[1],
        ffn_pieces[2].reshape(model_width, hidden_width),
        ffn_pieces[3],
        ffn_pieces[4].reshape(hidden_width, model_width),
        ffn_pieces[5],
    )
    grad_tokens, ffn_factors, ffn_small, attn_factors, attn_small = backward(
        stored_state, cotangent, attn_again, ffn_again
    )
    second_normed, grad_before_low, active, grad_final_low = ffn_factors
    first_normed, grad_packed, context, grad_middle_low = attn_factors
    ffn_parts = (
        lax.psum_scatter(ffn_small[0], "dp", scatter_dimension=0, tiled=True),
        lax.psum_scatter(ffn_small[1], "dp", scatter_dimension=0, tiled=True),
        lax.psum_scatter(
            flatten_lanes(transposed_left(second_normed, grad_before_low)),
            "dp",
            scatter_dimension=0,
            tiled=True,
        ),
        lax.psum_scatter(ffn_small[2], "dp", scatter_dimension=0, tiled=True),
        lax.psum_scatter(
            flatten_lanes(transposed_left(active, grad_final_low)),
            "dp",
            scatter_dimension=0,
            tiled=True,
        ),
        lax.psum_scatter(ffn_small[3], "dp", scatter_dimension=0, tiled=True),
    )
    ffn_shards = (
        ffn_parts[0],
        ffn_parts[1],
        ffn_parts[2].reshape(-1, hidden_width),
        ffn_parts[3],
        ffn_parts[4].reshape(-1, model_width),
        ffn_parts[5],
    )
    attn_parts = (
        lax.psum_scatter(attn_small[0], "dp", scatter_dimension=0, tiled=True),
        lax.psum_scatter(attn_small[1], "dp", scatter_dimension=0, tiled=True),
        lax.psum_scatter(
            flatten_lanes(transposed_left(first_normed, grad_packed)),
            "dp",
            scatter_dimension=0,
            tiled=True,
        ),
        lax.psum_scatter(attn_small[2], "dp", scatter_dimension=0, tiled=True),
        lax.psum_scatter(attn_small[3], "dp", scatter_dimension=0, tiled=True),
        lax.psum_scatter(
            flatten_lanes(transposed_left(context, grad_middle_low)),
            "dp",
            scatter_dimension=0,
            tiled=True,
        ),
        lax.psum_scatter(attn_small[4], "dp", scatter_dimension=0, tiled=True),
    )
    attn_shards = (
        attn_parts[0],
        attn_parts[1],
        attn_parts[2].reshape(-1, 3 * model_width),
        attn_parts[3],
        attn_parts[4],
        attn_parts[5].reshape(-1, model_width),
        attn_parts[6],
    )
    return (
        layer_output,
        grad_tokens,
        attn_shards[0],
        attn_shards[1],
        attn_shards[2],
        attn_shards[3],
        attn_shards[4],
        attn_shards[5],
        attn_shards[6],
        ffn_shards[0],
        ffn_shards[1],
        ffn_shards[2],
        ffn_shards[3],
        ffn_shards[4],
        ffn_shards[5],
    )


def solution(mesh):
    in_specs = (
        P("dp", None),
        P("dp", None),
        P("dp", None),
        P("dp"),
        P("dp"),
        P("dp", None),
        P("dp"),
        P("dp"),
        P("dp", None),
        P("dp"),
        P("dp"),
        P("dp"),
        P("dp", None),
        P("dp"),
        P("dp", None),
        P("dp"),
    )
    out_specs = (
        P("dp", None),
        P("dp", None),
        P("dp"),
        P("dp"),
        P("dp", None),
        P("dp"),
        P("dp"),
        P("dp", None),
        P("dp"),
        P("dp"),
        P("dp"),
        P("dp", None),
        P("dp"),
        P("dp", None),
        P("dp"),
    )
    return jax.shard_map(
        on_device, mesh=mesh, in_specs=in_specs, out_specs=out_specs, check_vma=False
    )
```

profile of v0, /device:TPU:13, one launch (start us, length us, event | category | flops | bytes accessed | tf_op | source)
XLA Modules:
  0.0 1015.1 jit_solution(6568556439377128779)
XLA Ops:
  7.3 1.6 reshape.271
  9.0 1.7 reshape.264
  10.8 1.8 reshape.273
  12.6 1.8 reshape.275
  14.7 0.6 slice.15
  17.1 40.2 %all-reduce.18 = (bf16[1024]{0:T(1024)(128)(2,1)S(1)}, bf16[1024]{0:T(1024)(128)(2,1)S(1)}, bf16[1024]{0:T(1024)(128)(2,1)S(1)}, bf16[1024]{0:T(1024)(128)(2,1)S...) all-reduce(bf16[1024]{0:T(1024)(128)(2,1)S(1)} %dynamic-update-slic, ...), channel_id=1, replica_groups=mesh['dp'=32] {'dp'}, use_global_device_ids=true, to_apply=%add.1 | all-reduce | flops 8192 | bytes 32768
  57.4 31.3 %all-gather = bf16[32,1,128]{2,1,0:T(2,128)(2,1)S(1)} all-gather(bf16[1,1,128]{2,1,0:T(2,128)(2,1)S(1)} %bitcast.58), channel_id=1, replica_groups=mesh['dp'=32] {'dp'}, dimensions={0}, use_global_device_ids=true | all-gather | bytes 8448 | tf_op jit(solution)/shard_map/all_gather | solution.py:260
  88.7 0.7 compare_convert_fusion.1
  89.8 0.6 compare_select_fusion
  90.5 3.0 reshape.272
  93.6 47.5 %all-gather.6.cloned.1.call-done = bf16[24576,128]{1,0:T(8,128)(2,1)} async-done(((bf16[768,128]{1,0:T(8,128)(2,1)}), bf16[24576,128]{1,0:T(8,128)(2,1)}) %all-gather.6.cloned.1.call-update) | async-done | bytes 6291472 | tf_op jit(solution)/shard_map/all_gather | solution.py:229
  141.1 10.3 %reshape.265 = bf16[1024,3072]{1,0:T(8,128)(2,1)} reshape(bf16[24576,128]{1,0:T(8,128)(2,1)} %all-gather.6.cloned.1.call-done) | data formatting | bytes 12582912 | tf_op jit(solution)/shard_map/reshape | solution.py:238
  151.4 4.0 fusion.68
  157.9 62.3 %all-gather.10.cloned.1.call-done = bf16[32768,128]{1,0:T(8,128)(2,1)} async-done(((bf16[1024,128]{1,0:T(8,128)(2,1)}), bf16[32768,128]{1,0:T(8,128)(2,1)}) %all-gather.10.cloned.1.call-update) | async-done | bytes 8388624 | tf_op jit(solution)/shard_map/all_gather | solution.py:259
  220.2 13.4 %reshape.274 = bf16[1024,4096]{1,0:T(8,128)(2,1)} reshape(bf16[32768,128]{1,0:T(8,128)(2,1)} %all-gather.10.cloned.1.call-done) | data formatting | bytes 16777216 | tf_op jit(solution)/shard_map/reshape | solution.py:267
  233.6 6.1 convolution_add_fusion
  239.7 59.5 %all-gather.12.cloned.1.call-done = bf16[32768,128]{1,0:T(8,128)(2,1)} async-done(((bf16[1024,128]{1,0:T(8,128)(2,1)}), bf16[32768,128]{1,0:T(8,128)(2,1)}) %all-gather.12.cloned.1.call-update) | async-done | bytes 8388624 | tf_op jit(solution)/shard_map/all_gather | solution.py:261
  299.2 13.3 %reshape.276 = bf16[4096,1024]{1,0:T(8,128)(2,1)} reshape(bf16[32768,128]{1,0:T(8,128)(2,1)} %all-gather.12.cloned.1.call-done) | data formatting | bytes 16777216 | tf_op jit(solution)/shard_map/reshape | solution.py:269
  312.5 8.2 fusion.80
  320.7 6.8 multiply_reduce_fusion.1
  327.8 2.7 fusion.48
  330.5 5.0 reshape.283
  335.8 2.5 convolution_convert_fusion.1
  338.3 1.2 copy.63
  339.5 2.3 fusion.81
  341.8 2.0 convolution_convert_fusion
  343.8 2.2 fusion.75
  346.6 6.5 fusion.44
  353.2 13.8 %reshape.281 = f32[24576,128]{1,0:T(8,128)} reshape(f32[1024,3072]{1,0:T(8,128)} %fusion.44) | data formatting | bytes 25165824 | tf_op jit(solution)/shard_map/reshape | solution.py:49
  367.1 1.5 copy-done.3
  368.6 9.1 fusion.51
  377.7 18.0 %reshape.287 = f32[32768,128]{1,0:T(8,128)} reshape(f32[4096,1024]{1,0:T(8,128)} %fusion.51) | data formatting | bytes 33554432 | tf_op jit(solution)/shard_map/reshape | solution.py:49
  396.1 9.4 fusion.32
  405.5 18.1 %reshape.285 = f32[32768,128]{1,0:T(8,128)} reshape(f32[1024,4096]{1,0:T(8,128)} %fusion.32) | data formatting | bytes 33554432 | tf_op jit(solution)/shard_map/reshape | solution.py:49
  423.7 5.4 fusion.72
  429.5 1.2 fusion.36
  430.6 38.7 %all-reduce.17 = (f32[1024]{0:T(1024)S(1)}, f32[1024]{0:T(1024)S(1)}, f32[1024]{0:T(1024)S(1)}, f32[1024]{0:T(1024)S(1)}, f32[1024]{0:T(1024)S(1)}, /*index=5*/f...) all-reduce(f32[1024]{0:T(1024)S(1)} %get-tuple-element.17, ...), channel_id=2, replica_groups=mesh['dp'=32] {'dp'}, use_global_device_ids=true, to_apply=%region_14.15.clone | all-reduce | flops 12288 | bytes 98304
  469.3 0.6 dynamic-slice
  470.5 0.6 dynamic-slice.2
  474.0 0.6 dynamic-slice.7
  474.6 5.6 fusion.13
  480.2 1.6 reshape.284
  481.8 149.2 %reduce-scatter.5.cloned.1.call-done = f32[768,128]{1,0:T(8,128)} async-done(((f32[24576,128]{1,0:T(8,128)}), f32[768,128]{1,0:T(8,128)}) %reduce-scatter.5.cloned.1.call-update) | async-done | bytes 393232 | tf_op jit(solution)/shard_map/reduce_scatter | solution.py:383
  630.9 1.8 reshape.282
  632.7 186.6 %reduce-scatter.11.cloned.1.call-done = f32[1024,128]{1,0:T(8,128)} async-done(((f32[32768,128]{1,0:T(8,128)}), f32[1024,128]{1,0:T(8,128)}) %reduce-scatter.11.cloned.1.call-update) | async-done | bytes 524304 | tf_op jit(solution)/shard_map/reduce_scatter | solution.py:364
  819.4 1.9 reshape.288
  821.3 185.0 %reduce-scatter.9.cloned.1.call-done = f32[1024,128]{1,0:T(8,128)} async-done(((f32[32768,128]{1,0:T(8,128)}), f32[1024,128]{1,0:T(8,128)}) %reduce-scatter.9.cloned.1.call-update) | async-done | bytes 524304 | tf_op jit(solution)/shard_map/reduce_scatter | solution.py:357
  1006.3 1.9 reshape.286
  (133 shorter events, 10.9 us)
Async XLA Ops:
  7.2 7.3 copy-start.19
  7.2 8.1 copy-start.20
  7.2 8.2 copy-start.21
  7.2 8.5 copy-start.22
  7.2 8.7 copy-start.23
  7.2 8.9 copy-start.24
  7.2 9.2 copy-start.25
  7.3 9.4 copy-start.26
  7.3 9.6 copy-start.27
  7.3 50.1 %copy-start.18 = (bf16[128]{0:T(256)(128)(2,1)S(1)}, bf16[128]{0:T(256)(128)(2,1)}, u32[]{:S(2)}) copy-start(bf16[128]{0:T(256)(128)(2,1)} %param.29) | copy-start | bytes 772
  7.3 82.1 %copy-start.2 = (bf16[128,1024]{1,0:T(8,128)(2,1)S(1)}, bf16[128,1024]{1,0:T(8,128)(2,1)}, u32[]{:S(2)}) copy-start(bf16[128,1024]{1,0:T(8,128)(2,1)} %param.16) | copy-start | bytes 786436
  7.3 83.2 %all-gather.8.cloned.1.call-start = ((), (), s32[]{:S(2)}) async-start(), calls=%async_computation.5 | async-start | bytes 2162688 | tf_op jit(solution)/shard_map/all_gather | solution.py:232
  8.9 132.2 %all-gather.6.cloned.1.call-start = ((), (), s32[]{:S(2)}) async-start(), calls=%async_computation.4 | async-start | bytes 6488064 | tf_op jit(solution)/shard_map/all_gather | solution.py:229
  10.7 209.5 %all-gather.10.cloned.1.call-start = ((), (), s32[]{:S(2)}) async-start(), calls=%async_computation.6 | async-start | bytes 8650752 | tf_op jit(solution)/shard_map/all_gather | solution.py:259
  12.6 286.6 %all-gather.12.cloned.1.call-start = ((), (), s32[]{:S(2)}) async-start(), calls=%async_computation.7 | async-start | bytes 8650752 | tf_op jit(solution)/shard_map/all_gather | solution.py:261
  14.4 465.8 %reduce-scatter.7.cloned.1.call-start = ((), (), s32[]{:S(2)}) async-start(), calls=%async_computation.9 | async-start | bytes 4325376 | tf_op jit(solution)/shard_map/reduce_scatter | solution.py:391
  155.7 1.2 copy-start.14
  155.9 1.1 copy-start.12
  156.1 0.9 copy-start.8
  156.5 1.1 copy-start
  157.0 0.7 copy-start.9
  239.7 72.8 %copy-start.4 = (bf16[128,1024]{1,0:T(8,128)(2,1)S(1)}, bf16[128,1024]{1,0:T(8,128)(2,1)}, u32[]{:S(2)}) copy-start(bf16[128,1024]{1,0:T(8,128)(2,1)} %param.18) | copy-start | bytes 786436
  320.7 6.8 copy-start.7
  320.7 7.1 copy-start.5
  320.7 7.1 copy-start.10
  335.5 295.4 %reduce-scatter.5.cloned.1.call-start = ((), (), s32[]{:S(2)}) async-start(), calls=%async_computation.8 | async-start | bytes 12976128 | tf_op jit(solution)/shard_map/reduce_scatter | solution.py:383
  338.3 3.5 copy-start.1
  338.3 3.5 copy-start.15
  338.3 5.6 copy-start.13
  343.8 9.3 copy-start.16
  346.1 7.1 copy-start.17
  346.6 6.6 copy-start.11
  367.0 1.6 copy-start.3
  367.0 452.4 %reduce-scatter.11.cloned.1.call-start = ((), (), s32[]{:S(2)}) async-start(), calls=%async_computation.11 | async-start | bytes 17301504 | tf_op jit(solution)/shard_map/reduce_scatter | solution.py:364
  395.8 610.5 %reduce-scatter.9.cloned.1.call-start = ((), (), s32[]{:S(2)}) async-start(), calls=%async_computation.10 | async-start | bytes 17301504 | tf_op jit(solution)/shard_map/reduce_scatter | solution.py:357
  423.7 5.8 copy-start.6
Sparse Core Ops, SparseCore 0:
  11.5 56.9 all-gather.7
  72.0 69.0 all-gather.5
  144.5 75.5 all-gather.9
  223.5 75.6 all-gather.11
  335.6 107.8 reduce-scatter.6
  449.4 181.4 reduce-scatter.4
  633.2 186.1 reduce-scatter.10
  821.7 184.5 reduce-scatter.8
where the time goes:
time: 1020 us
  waiting for transfers between devices  690 us (68%)
  local copies, waits for them, and re-layouts  120 us (12%)
  blocking collectives  110 us (11%)
  matrix products  74.5 us (7%)
  between operations  14.7 us (1%)
    reduce_scatter x1, waiting for transfers between devices, on_device(): lax.psum_scatter(flatten_lanes(transposed_left(active, grad_final_low)),...  187 us
    reduce_scatter x1, waiting for transfers between devices, on_device(): lax.psum_scatter(flatten_lanes(transposed_left(second_normed, grad_before...  185 us
    reduce_scatter x1, waiting for transfers between devices, on_device(): lax.psum_scatter(flatten_lanes(transposed_left(first_normed, grad_packed)...  149 us
    unnamed x2, blocking collectives  78.9 us
    all_gather x1, waiting for transfers between devices, gather_feedforward(): lax.all_gather(flatten_lanes(expand_weight), 'dp', axis=0, tiled=True)  62.3 us
    reshape x8, local copies, waits for them, and re-layouts, flatten_lanes(): return matrix.reshape(-1, 128)  61.7 us
    all_gather x1, waiting for transfers between devices, gather_feedforward(): lax.all_gather(flatten_lanes(reduce_weight), 'dp', axis=0, tiled=True)  59.5 us
    all_gather x1, waiting for transfers between devices, gather_attention(): lax.all_gather(flatten_lanes(joint_weight), 'dp', axis=0, tiled=True)  47.5 us
  transfers between devices with their start and end apart: 8, of which 6 were waited for; matrix products, arithmetic and copies ran while one was open for 16% of the time, Pallas kernels for 0%

commit v1 on v0

--- a/solution.py
+++ b/solution.py
@@ -43,10 +43,6 @@
     return lax.dot_general(
         first_op, second_op, (((1,), (1,)), ((), ())), preferred_element_type=jnp.float32
     )
-
-
-def flatten_lanes(matrix):
-    return matrix.reshape(-1, 128)
 
 
 def slot_mask(lengths_row, row_count):
@@ -213,62 +209,68 @@
     return (grad_tokens, ffn_factors, ffn_small, attn_factors, attn_small)
 
 
-def gather_attention(
-    norm1_gain,
-    norm1_shift,
-    joint_weight,
-    query_bias,
-    value_bias,
-    output_weight,
-    output_bias,
-    model_width,
-):
-    pieces = (
-        lax.all_gather(norm1_gain, "dp", axis=0, tiled=True),
-        lax.all_gather(norm1_shift, "dp", axis=0, tiled=True),
-        lax.all_gather(flatten_lanes(joint_weight), "dp", axis=0, tiled=True),
-        lax.all_gather(query_bias, "dp", axis=0, tiled=True),
-        lax.all_gather(value_bias, "dp", axis=0, tiled=True),
-        lax.all_gather(flatten_lanes(output_weight), "dp", axis=0, tiled=True),
-        lax.all_gather(output_bias, "dp", axis=0, tiled=True),
-    )
-    return (
-        pieces[0],
-        pieces[1],
-        pieces[2].reshape(model_width, 3 * model_width),
-        pieces[3],
-        pieces[4],
-        pieces[5].reshape(model_width, model_width),
-        pieces[6],
-    )
-
-
-def gather_feedforward(
-    norm2_gain,
-    norm2_shift,
-    expand_weight,
-    expand_bias,
-    reduce_weight,
-    reduce_bias,
-    model_width,
-    hidden_width,
-):
-    pieces = (
-        lax.all_gather(norm2_gain, "dp", axis=0, tiled=True),
-        lax.all_gather(norm2_shift, "dp", axis=0, tiled=True),
-        lax.all_gather(flatten_lanes(expand_weight), "dp", axis=0, tiled=True),
-        lax.all_gather(expand_bias, "dp", axis=0, tiled=True),
-        lax.all_gather(flatten_lanes(reduce_weight), "dp", axis=0, tiled=True),
-        lax.all_gather(reduce_bias, "dp", axis=0, tiled=True),
-    )
-    return (
-        pieces[0],
-        pieces[1],
-        pieces[2].reshape(model_width, hidden_width),
-        pieces[3],
-        pieces[4].reshape(hidden_width, model_width),
-        pieces[5],
-    )
+def split_blocks(matrix, block_rows):
+    return jnp.concatenate(
+        [
+            matrix[start : start + block_rows]
+            for start in range(0, matrix.shape[0], block_rows)
+        ],
+        axis=1,
+    )
+
+
+def small_width(count, block_rows):
+    return 128 * (-(-count // (block_rows * 128)))
+
+
+def gather_params(matrices, vectors):
+    block_rows = matrices[0].shape[0]
+    lengths = [vector.shape[0] for vector in vectors]
+    width = small_width(sum(lengths), block_rows)
+    flat = jnp.concatenate(
+        list(vectors) + [jnp.zeros((width * block_rows - sum(lengths),), vectors[0].dtype)]
+    )
+    packed = jnp.concatenate(list(matrices) + [flat.reshape(block_rows, width)], axis=1)
+    whole = lax.all_gather(packed, "dp", axis=0, tiled=True)
+    columns, at = [], 0
+    for matrix in matrices:
+        columns.append(whole[:, at : at + matrix.shape[1]])
+        at += matrix.shape[1]
+    small = whole[:, at:].reshape(-1, block_rows * width)
+    pieces, at = [], 0
+    for length in lengths:
+        pieces.append(small[:, at : at + length].reshape(-1))
+        at += length
+    return columns, pieces
+
+
+def scatter_sum(matrices, vectors):
+    low = [matrix.astype(jnp.bfloat16) for matrix in matrices]
+    devices = lax.axis_size("dp")
+    block_rows = matrices[0].shape[0] // devices
+    lengths = [vector.shape[0] // devices for vector in vectors]
+    if vectors:
+        width = small_width(sum(lengths), block_rows)
+        flat = jnp.concatenate(
+            [vector.reshape(devices, -1) for vector in vectors]
+            + [jnp.zeros((devices, width * block_rows - sum(lengths)), jnp.float32)],
+            axis=1,
+        )
+        low.append(flat.astype(jnp.bfloat16).reshape(devices * block_rows, width))
+    shard = lax.psum_scatter(
+        jnp.concatenate(low, axis=1), "dp", scatter_dimension=0, tiled=True
+    )
+    columns, at = [], 0
+    for matrix in matrices:
+        columns.append(shard[:, at : at + matrix.shape[1]].astype(jnp.float32))
+        at += matrix.shape[1]
+    pieces = []
+    if vectors:
+        small, at = shard[:, at:].reshape(-1), 0
+        for length in lengths:
+            pieces.append(small[at : at + length].astype(jnp.float32))
+            at += length
+    return columns, pieces
 
 
 def on_device(
@@ -291,136 +293,84 @@
 ):
     model_width = tokens.shape[1]
     hidden_width = expand_weight.shape[1]
-    attn_params = gather_attention(
-        norm1_gain,
-        norm1_shift,
-        joint_weight,
-        query_bias,
-        value_bias,
-        output_weight,
-        output_bias,
-        model_width,
-    )
-    ffn_params = gather_feedforward(
-        norm2_gain,
-        norm2_shift,
-        expand_weight,
-        expand_bias,
-        reduce_weight,
-        reduce_bias,
-        model_width,
-        hidden_width,
-    )
+    devices = lax.axis_size("dp")
+    block_rows = joint_weight.shape[0]
+    blocks = reduce_weight.shape[0] // block_rows
+    matrices, vectors = gather_params(
+        (joint_weight, output_weight, expand_weight, split_blocks(reduce_weight, block_rows)),
+        (
+            norm1_gain,
+            norm1_shift,
+            query_bias,
+            value_bias,
+            output_bias,
+            norm2_gain,
+            norm2_shift,
+            expand_bias,
+            reduce_bias,
+        ),
+    )
+    reduce_whole = (
+        matrices[3]
+        .reshape(devices, block_rows, blocks, model_width)
+        .transpose(0, 2, 1, 3)
+        .reshape(hidden_width, model_width)
+    )
+    attn_params = (
+        vectors[0],
+        vectors[1],
+        matrices[0],
+        vectors[2],
+        vectors[3],
+        matrices[1],
+        vectors[4],
+    )
+    ffn_params = (vectors[5], vectors[6], matrices[2], vectors[7], reduce_whole, vectors[8])
     layer_output, stored_state = forward(tokens, lengths[0], attn_params, ffn_params)
-    attn_pieces = (
-        lax.all_gather(norm1_gain, "dp", axis=0, tiled=True),
-        lax.all_gather(norm1_shift, "dp", axis=0, tiled=True),
-        lax.all_gather(flatten_lanes(joint_weight), "dp", axis=0, tiled=True),
-        lax.all_gather(query_bias, "dp", axis=0, tiled=True),
-        lax.all_gather(value_bias, "dp", axis=0, tiled=True),
-        lax.all_gather(flatten_lanes(output_weight), "dp", axis=0, tiled=True),
-        lax.all_gather(output_bias, "dp", axis=0, tiled=True),
-    )
-    attn_again = (
-        attn_pieces[0],
-        attn_pieces[1],
-        attn_pieces[2].reshape(model_width, 3 * model_width),
-        attn_pieces[3],
-        attn_pieces[4],
-        attn_pieces[5].reshape(model_width, model_width),
-        attn_pieces[6],
-    )
-    ffn_pieces = (
-        lax.all_gather(norm2_gain, "dp", axis=0, tiled=True),
-        lax.all_gather(norm2_shift, "dp", axis=0, tiled=True),
-        lax.all_gather(flatten_lanes(expand_weight), "dp", axis=0, tiled=True),
-        lax.all_gather(expand_bias, "dp", axis=0, tiled=True),
-        lax.all_gather(flatten_lanes(reduce_weight), "dp", axis=0, tiled=True),
-        lax.all_gather(reduce_bias, "dp", axis=0, tiled=True),
-    )
-    ffn_again = (
-        ffn_pieces[0],
-        ffn_pieces[1],
-        ffn_pieces[2].reshape(model_width, hidden_width),
-        ffn_pieces[3],
-        ffn_pieces[4].reshape(hidden_width, model_width),
-        ffn_pieces[5],
-    )
     grad_tokens, ffn_factors, ffn_small, attn_factors, attn_small = backward(
-        stored_state, cotangent, attn_again, ffn_again
+        stored_state, cotangent, attn_params, ffn_params
     )
     second_normed, grad_before_low, active, grad_final_low = ffn_factors
     first_normed, grad_packed, context, grad_middle_low = attn_factors
-    ffn_parts = (
-        lax.psum_scatter(ffn_small[0], "dp", scatter_dimension=0, tiled=True),
-        lax.psum_scatter(ffn_small[1], "dp", scatter_dimension=0, tiled=True),
-        lax.psum_scatter(
-            flatten_lanes(transposed_left(second_normed, grad_before_low)),
-            "dp",
-            scatter_dimension=0,
-            tiled=True,
+    grad_reduce = (
+        transposed_left(active, grad_final_low)
+        .astype(jnp.bfloat16)
+        .reshape(devices, blocks, block_rows, model_width)
+        .transpose(0, 2, 1, 3)
+        .reshape(devices * block_rows, blocks * model_width)
+    )
+    ffn_parts, unused_pieces = scatter_sum(
+        (transposed_left(second_normed, grad_before_low), grad_reduce), ()
+    )
+    attn_parts, small_parts = scatter_sum(
+        (
+            transposed_left(first_normed, grad_packed),
+            transposed_left(context, grad_middle_low),
         ),
-        lax.psum_scatter(ffn_small[2], "dp", scatter_dimension=0, tiled=True),
-        lax.psum_scatter(
-            flatten_lanes(transposed_left(active, grad_final_low)),
-            "dp",
-            scatter_dimension=0,
-            tiled=True,
-        ),
-        lax.psum_scatter(ffn_small[3], "dp", scatter_dimension=0, tiled=True),
-    )
-    ffn_shards = (
-        ffn_parts[0],
-        ffn_parts[1],
-        ffn_parts[2].reshape(-1, hidden_width),
-        ffn_parts[3],
-        ffn_parts[4].reshape(-1, model_width),
-        ffn_parts[5],
-    )
-    attn_parts = (
-        lax.psum_scatter(attn_small[0], "dp", scatter_dimension=0, tiled=True),
-        lax.psum_scatter(attn_small[1], "dp", scatter_dimension=0, tiled=True),
-        lax.psum_scatter(
-            flatten_lanes(transposed_left(first_normed, grad_packed)),
-            "dp",
-            scatter_dimension=0,
-            tiled=True,
-        ),
-        lax.psum_scatter(attn_small[2], "dp", scatter_dimension=0, tiled=True),
-        lax.psum_scatter(attn_small[3], "dp", scatter_dimension=0, tiled=True),
-        lax.psum_scatter(
-            flatten_lanes(transposed_left(context, grad_middle_low)),
-            "dp",
-            scatter_dimension=0,
-            tiled=True,
-        ),
-        lax.psum_scatter(attn_small[4], "dp", scatter_dimension=0, tiled=True),
-    )
-    attn_shards = (
-        attn_parts[0],
-        attn_parts[1],
-        attn_parts[2].reshape(-1, 3 * model_width),
-        attn_parts[3],
-        attn_parts[4],
-        attn_parts[5].reshape(-1, model_width),
-        attn_parts[6],
+        attn_small + ffn_small,
+    )
+    grad_reduce_shard = (
+        ffn_parts[1]
+        .reshape(block_rows, blocks, model_width)
+        .transpose(1, 0, 2)
+        .reshape(blocks * block_rows, model_width)
     )
     return (
         layer_output,
         grad_tokens,
-        attn_shards[0],
-        attn_shards[1],
-        attn_shards[2],
-        attn_shards[3],
-        attn_shards[4],
-        attn_shards[5],
-        attn_shards[6],
-        ffn_shards[0],
-        ffn_shards[1],
-        ffn_shards[2],
-        ffn_shards[3],
-        ffn_shards[4],
-        ffn_shards[5],
+        small_parts[0],
+        small_parts[1],
+        attn_parts[0],
+        small_parts[2],
+        small_parts[3],
+        attn_parts[1],
+        small_parts[4],
+        small_parts[5],
+        small_parts[6],
+        ffn_parts[0],
+        small_parts[7],
+        grad_reduce_shard,
+        small_parts[8],
     )
 
 

time: 1020 us -> 598 us (0.59)
  waiting for transfers between devices: 690 us -> 424 us
  blocking collectives: 110 us -> 0 us
  local copies, waits for them, and re-layouts: 120 us -> 74.5 us
  other arithmetic: 4.33 us -> 24.5 us
  matrix products: 74.5 us -> 58.6 us
    reduce_scatter x4 -> x2, waiting for transfers between devices: 521 us -> 272 us  [scatter_sum(): lax.psum_scatter(jnp.concatenate(low, axis=1), 'dp', scatter_dimension=0,...]
    reshape x16 -> x14, local copies, waits for them, and re-layouts: 109 us -> 25.3 us  [the longest x1 14.5 us: on_device(): reduce_whole = matrices[3].reshape(devices, block_rows, blocks, model_wid...]
    unnamed x2 -> x0, blocking collectives: 78.9 us -> none
    all_gather x1 -> x0, blocking collectives: 31.3 us -> none  [gather_feedforward(): lax.all_gather(expand_bias, 'dp', axis=0, tiled=True)]
    all_gather x4 -> x1, waiting for transfers between devices: 169 us -> 153 us  [gather_params(): whole = lax.all_gather(packed, 'dp', axis=0, tiled=True)]
    dot_general x4, matrix products: 27.8 us -> 13.2 us  [transposed_left(): lax.dot_general(first_op, second_op, (((0,), (0,)), ((), ())), preferred_...]
    concatenate x0 -> x2, other arithmetic: none -> 13.8 us  [scatter_sum(): jnp.concatenate(low, axis=1)]
    unnamed x81 -> x36, local copies, waits for them, and re-layouts: 8.85 us -> 21 us
  transfers between devices with their start and end apart: 8 -> 3, of which waited for: 6 -> 3; matrix products, arithmetic and copies ran while one was open for 16% -> 8% of each run, Pallas kernels for 0% -> 0%
where the time goes in v1:
time: 598 us; the launch traced here: 596 us
  waiting for transfers between devices  424 us (71%)
  local copies, waits for them, and re-layouts  74.5 us (12%)
  matrix products  58.6 us (10%)
  other arithmetic  24.5 us (4%)
  between operations  14.1 us (2%)
    reduce_scatter x2, waiting for transfers between devices, scatter_sum(): lax.psum_scatter(jnp.concatenate(low, axis=1), 'dp', scatter_dimension=0,...  272 us
    all_gather x1, waiting for transfers between devices, gather_params(): whole = lax.all_gather(packed, 'dp', axis=0, tiled=True)  153 us
    unnamed x36, local copies, waits for them, and re-layouts  21 us
    dot_general x4, matrix products, transposed_right(): lax.dot_general(first_op, second_op, (((1,), (1,)), ((), ())), preferred_...  19.6 us
    reshape x1, local copies, waits for them, and re-layouts, on_device(): reduce_whole = matrices[3].reshape(devices, block_rows, blocks, model_wid...  14.5 us
    concatenate x2, other arithmetic, scatter_sum(): jnp.concatenate(low, axis=1)  13.8 us
    dot_general x4, matrix products, transposed_left(): lax.dot_general(first_op, second_op, (((0,), (0,)), ((), ())), preferred_...  13.2 us
  transfers between devices with their start and end apart: 3, of which 3 were waited for; matrix products, arithmetic and copies ran while one was open for 8% of the time, Pallas kernels for 0%

profile of v1, /device:TPU:13, one launch (start us, length us, event | category | flops | bytes accessed | tf_op | source)
XLA Modules:
  0.0 596.2 jit_solution(6993355972113359031)
XLA Ops:
  7.2 1.0 constant_dynamic-update-slice_fusion.3
  8.2 0.8 constant_dynamic-update-slice_fusion.2
  9.1 1.0 constant_dynamic-update-slice_fusion.1
  10.0 0.8 slice_dynamic-update-slice_fusion.3
  10.9 0.8 slice_dynamic-update-slice_fusion.2
  11.7 0.8 slice_dynamic-update-slice_fusion.1
  12.6 0.8 slice_dynamic-update-slice_fusion
  13.4 6.1 %concatenate.20 = bf16[4096]{0:T(1024)(128)(2,1)S(1)} concatenate(bf16[32]{0:T(256)(128)(2,1)} %param.19, bf16[32]{0:T(256)(128)(2,1)} %param.20, bf16[32]{0:T(256)(128)(2,1)} %param.22, bf16[32]{0:T(256)(128)(2,1)} %param.23, bf16[32]{0:T(256)(128)(2,1)} %param.25, bf16[32]{0:T(256)(128)(2,1)} %param.26, bf16[32]{0:T(256)(128)(2,1)} %param.27, bf16[128]{0:T(256)(128)(2,1)} %param.29, ...), dimensions={0} | concatenate | bytes 16384 | tf_op jit(solution)/shard_map/concatenate | solution.py:230
  19.5 1.0 copy-done.4
  20.8 0.6 slice.120
  21.3 0.6 compare_convert_fusion.1
  22.4 0.7 compare_select_fusion
  23.2 152.6 %all-gather.2.cloned.1.call-done = bf16[1024,12416]{1,0:T(8,128)(2,1)} async-done(((bf16[32,12416]{1,0:T(8,128)(2,1)}), bf16[1024,12416]{1,0:T(8,128)(2,1)}) %all-gather.2.cloned.1.call-update) | async-done | bytes 25427984 | tf_op jit(solution)/shard_map/all_gather | solution.py:234
  175.8 1.0 slice.146
  177.4 3.9 fusion.7
  182.6 7.7 %slice.161 = bf16[1024,4096]{1,0:T(8,128)(2,1)} slice(bf16[1024,12416]{1,0:T(8,128)(2,1)} %all-gather.2.cloned.1.call-done), slice={[0:1024], [8192:12288]} | slice | bytes 16777216 | tf_op jit(solution)/shard_map/slice | solution.py:237
  190.3 14.5 %reshape.354 = bf16[32,32,4,1024]{3,2,1,0:T(4,128)(2,1)} reshape(bf16[1024,4096]{1,0:T(8,128)(2,1)} %slice.161) | data formatting | bytes 16777216 | tf_op jit(solution)/shard_map/reshape | solution.py:315
  204.8 10.3 %copy.73 = bf16[32,4,32,1024]{3,2,1,0:T(8,128)(2,1)} copy(bf16[32,4,32,1024]{3,1,2,0:T(4,128)(2,1)} %bitcast.55) | data formatting | bytes 16777216 | tf_op jit(solution)/shard_map/transpose | solution.py:316
  215.5 2.3 fusion.94
  218.1 4.9 fusion.9
  223.0 4.6 fusion.97
  227.6 6.8 %multiply_reduce_fusion.1 = (bf16[1024]{0:T(1024)(128)(2,1)S(1)}, f32[128]{0:T(128)S(1)}, bf16[1024]{0:T(1024)(128)(2,1)S(1)}, f32[128,1024]{1,0:T(8,128)S(1)}) fusion(f32[128,1024]{1,0:T(8,128)S(1)} %get-tuple-element.54, f32[128]{0:T(128)S(1)} %fusion.80, f32[128]{0:T(128)S(1)} %broadcast_multiply_fusion, f32[1024]{0:T(1024)S(1)} %reshape.380, ...), kind=kOutput, calls=%fused_computation.73 | convolution fusion | flops 1074788224 | bytes 10495488 | tf_op jit(solution)/shard_map/dot_general | solution.py:43
  234.7 3.1 fusion.34
  237.8 1.1 copy.74
  238.9 1.2 fusion.91
  240.1 1.3 fusion.98
  241.4 2.1 convolution_convert_fusion.4
  243.5 2.8 fusion.92
  246.3 2.2 convolution_convert_fusion.3
  248.5 4.6 convolution_convert_fusion.2
  253.1 5.1 fusion.89
  258.5 1.2 fusion.57
  260.6 7.2 %pad_maximum_fusion.1 = bf16[1024,4224]{1,0:T(8,128)(2,1)} fusion(bf16[1024,128]{1,0:T(8,128)(2,1)S(1)} %convert_element_type.245, bf16[1024,1024]{1,0:T(8,128)(2,1)} %convolution_convert_fusion.3, bf16[1024,3072]{1,0:T(8,128)(2,1)} %convolution_convert_fusion.2), kind=kLoop, calls=%fused_computation.2 | loop fusion | flops 25952256 | bytes 17301504 | tf_op jit(solution)/shard_map/concatenate | solution.py:261
  267.8 4.0 convolution_convert_fusion
  271.9 7.9 %copy.79 = bf16[32,4,32,1024]{3,1,2,0:T(4,128)(2,1)} copy(bf16[32,4,32,1024]{3,2,1,0:T(8,128)(2,1)S(1)} %bitcast.54) | data formatting | bytes 16777216 | tf_op jit(solution)/shard_map/reshape | solution.py:338
  279.8 12.5 %copy.86 = bf16[128,8,4,1024]{3,1,2,0:T(8,128)(2,1)} copy(bf16[128,8,4,1024]{3,2,1,0:T(4,128)(2,1)} %bitcast.56) | data formatting | bytes 16777216
  292.3 2.5 convolution_convert_fusion.1
  294.8 1.3 copy-done
  296.1 6.6 %pad_maximum_fusion = bf16[1024,8192]{1,0:T(8,128)(2,1)} fusion(bf16[1024,4096]{1,0:T(8,128)(2,1)S(1)} %bitcast.57, bf16[1024,4096]{1,0:T(8,128)(2,1)S(1)} %convolution_convert_fusion.1), kind=kLoop, calls=%fused_computation.1 | loop fusion | flops 33554432 | bytes 33554432 | tf_op jit(solution)/shard_map/concatenate | solution.py:261
  302.8 6.7 %fusion.33 = bf16[128,1024]{1,0:T(8,128)(2,1)} fusion(f32[128,1024]{1,0:T(8,128)S(1)} %get-tuple-element.54, bf16[4096,1024]{1,0:T(8,128)(2,1)} %bitcast.58, f32[1024]{0:T(1024)S(1)} %reshape.383, f32[128,4096]{1,0:T(8,128)} %copy-done.2), kind=kOutput, calls=%fused_computation.42 | convolution fusion | flops 1078853632 | bytes 11276288 | tf_op jit(solution)/shard_map/dot_general | solution.py:115
  309.4 88.6 %reduce-scatter.3.cloned.1.call-done = bf16[32,4224]{1,0:T(8,128)(2,1)} async-done(((bf16[1024,4224]{1,0:T(8,128)(2,1)}), bf16[32,4224]{1,0:T(8,128)(2,1)}) %reduce-scatter.3.cloned.1.call-update) | async-done | bytes 270352 | tf_op jit(solution)/shard_map/reduce_scatter | solution.py:260
  398.1 0.7 slice_bitcast_fusion
  399.3 0.6 slice_convert_fusion.13
  399.9 1.5 slice_convert_fusion.4
  401.4 1.7 slice_convert_fusion.3
  403.1 183.2 %reduce-scatter.5.cloned.1.call-done = bf16[32,8192]{1,0:T(8,128)(2,1)} async-done(((bf16[1024,8192]{1,0:T(8,128)(2,1)}), bf16[32,8192]{1,0:T(8,128)(2,1)}) %reduce-scatter.5.cloned.1.call-update) | async-done | bytes 524304 | tf_op jit(solution)/shard_map/reduce_scatter | solution.py:260
  586.3 1.9 slice_convert_fusion.1
  588.6 1.1 copy.80
  (84 shorter events, 5.9 us)
Async XLA Ops:
  7.2 13.4 %copy-start.11 = (s32[1,2]{1,0:T(1,128)S(1)}, s32[1,2]{1,0:T(1,128)}, u32[]{:S(2)}) copy-start(s32[1,2]{1,0:T(1,128)} %param.17) | copy-start | bytes 28
  7.2 14.9 %copy-start.1 = (bf16[128,1024]{1,0:T(8,128)(2,1)S(1)}, bf16[128,1024]{1,0:T(8,128)(2,1)}, u32[]{:S(2)}) copy-start(bf16[128,1024]{1,0:T(8,128)(2,1)} %param.16) | copy-start | bytes 786436
  7.2 168.6 %all-gather.2.cloned.1.call-start = ((), (), s32[]{:S(2)}) async-start(), calls=%async_computation.2 | async-start | bytes 26222592 | tf_op jit(solution)/shard_map/all_gather | solution.py:234
  19.5 1.0 copy-start.4
  20.5 377.5 %reduce-scatter.3.cloned.1.call-start = ((), (), s32[]{:S(2)}) async-start(), calls=%async_computation.3 | async-start | bytes 8921088 | tf_op jit(solution)/shard_map/reduce_scatter | solution.py:260
  181.8 8.5 %copy-start.8 = (bf16[128,1024]{0,1:T(8,128)(2,1)}, bf16[128,1024]{0,1:T(8,128)(2,1)S(1)}, u32[]{:S(2)}) copy-start(bf16[128,1024]{0,1:T(8,128)(2,1)S(1)} %copy.70) | copy-start | bytes 786436
  182.0 8.3 %copy-start.7 = (bf16[128,1024]{0,1:T(8,128)(2,1)}, bf16[128,1024]{0,1:T(8,128)(2,1)S(1)}, u32[]{:S(2)}) copy-start(bf16[128,1024]{0,1:T(8,128)(2,1)S(1)} %copy.71) | copy-start | bytes 786436
  215.5 7.4 %slice-start = ((s8[8388608]{0:T(1024)(128)(4,1)}), s8[4194304]{0:T(1024)(128)(4,1)S(1)}, s32[]{:S(2)}) async-start(s8[8388608]{0:T(1024)(128)(4,1)} %bitcast.59), calls=%async_computation.5 | async-start | bytes 8388608
  218.0 4.9 slice-start.1
  218.0 4.9 copy-start.3
  222.9 4.6 copy-start.2
  227.6 6.8 %copy-start.5 = (bf16[128,4096]{1,0:T(8,128)(2,1)}, bf16[128,4096]{1,0:T(8,128)(2,1)S(1)}, u32[]{:S(2)}) copy-start(bf16[128,4096]{1,0:T(8,128)(2,1)S(1)} %get-tuple-element.60) | copy-start | bytes 3145732
  246.3 2.2 copy-start.9
  246.3 2.2 copy-start.10
  267.8 318.6 %reduce-scatter.5.cloned.1.call-start = ((), (), s32[]{:S(2)}) async-start(), calls=%async_computation.4 | async-start | bytes 17301504 | tf_op jit(solution)/shard_map/reduce_scatter | solution.py:260
  279.8 12.5 %copy-start.6 = (bf16[128,4096]{1,0:T(8,128)(2,1)S(1)}, bf16[128,4096]{1,0:T(8,128)(2,1)}, u32[]{:S(2)}) copy-start(bf16[128,4096]{1,0:T(8,128)(2,1)} %copy-done.5) | copy-start | bytes 3145732
  292.3 3.7 copy-start
Sparse Core Ops, SparseCore 0:
  20.6 155.0 all-gather.1
  267.9 130.1 reduce-scatter.2
  400.4 185.9 reduce-scatter.4
